TPU v7x, 256 devices: a whole 4x4x8 slice. The times are simulated.
256 devices in a mesh: group: 8 (over y, core), blk: 32 (over x, z).
Axes of the slice: x: 4, y: 4, z: 8, core: 2. Of those that a mesh axis runs over, the one named last changes fastest.
Arguments:
- sep_rhs: float32 [8, 4096, 256], P('group', 'blk'), may hold values from -6 to 6
- sep_inv: bfloat16 [8, 32, 128, 128], P('group', 'blk'), as said below
- fac_values: bfloat16 [8, 512, 128, 128], P('group', 'blk'), may hold values from -0.09375 to 0.09375
- fac_src: int32 [8, 512], P('group', 'blk'), may hold values from 0 to 31, as said below
- fac_count: int32 [8, 32], P('group', 'blk'), may hold values from 8 to 16, as said below
- sub_rhs: bfloat16 [8, 131072, 256], P('group', 'blk'), may hold values from -6 to 6
- sub_inv: bfloat16 [8, 1024, 128, 128], P('group', 'blk'), as said below
- sub_coup: bfloat16 [8, 1024, 128, 128], P('group', 'blk'), may hold values from -0.09375 to 0.09375
Outputs:
- sep_sol: bfloat16 [8, 4096, 256], P('group', 'blk')
- sub_sol: bfloat16 [8, 131072, 256], P('group', 'blk')
Inputs may be any that keep to these rules, and one draw needn't show every extreme that they name: `fac_src`: each owner's 16 entries are distinct row blocks of the separator before. The first fac_count entries of an owner's slots are live; in every separator some owner has all 16 and some owner has 8. `sep_inv`: every block is lower triangular. `sub_inv`: every block is lower triangular.
All inputs are finite; a program needn't handle non-finite values.
Results may differ from a plain program's by a relative error of at most 0.015.
Values may be sent and summed in bfloat16 or wider, within the bound.
A program may use at most 64 MiB of HBM per device.

v0:
```python
import math

import jax
import jax.numpy as jnp
from jax import lax
from jax.sharding import PartitionSpec as P


def shifted(value, axis, steps):
    count = lax.axis_size(axis)
    first, last = (max(0, -steps), min(count, count - steps))
    return lax.ppermute(value, axis, [(source, source + steps) for source in range(first, last)])


def on_device(sep_rhs, sep_inv, fac_values, fac_src, fac_count, sub_rhs, sub_inv, sub_coup):
    block_rows = sub_inv.shape[2]
    column_total = sep_rhs.shape[2]
    sub_blocks = sub_inv.shape[1]
    rhs_blocks = sub_rhs[0].reshape(sub_blocks, block_rows, column_total)
    local_sol = jnp.einsum(
        "nab,nbr->nar", sub_inv[0], rhs_blocks, preferred_element_type=jnp.float32
    ).astype(jnp.bfloat16)
    lifted = jnp.einsum("nab,nbr->ar", sub_coup[0], local_sol, preferred_element_type=jnp.float32)
    reduced = sep_rhs[0] - lifted
    owners = lax.axis_size("blk")
    slots = fac_values.shape[1]
    factors = fac_values[0]
    sources = fac_src[0]
    live_count = fac_count[0, 0]
    step_size = math.gcd(8, slots)
    turn_count = (live_count + step_size - 1) // step_size
    diag_inverse = sep_inv[0, 0]
    group_count = lax.axis_size("group")

    def update(pieces):
        column_count = pieces.shape[1]
        chosen = pieces.reshape(owners, block_rows, column_count)[sources]

        def add_slots(turn_index, running):
            first_slot = turn_index * step_size
            part_factor = lax.dynamic_slice_in_dim(factors, first_slot, step_size, 0)
            part_solved = lax.dynamic_slice_in_dim(chosen, first_slot, step_size, 0)
            keep_mask = (first_slot + jnp.arange(step_size, dtype=jnp.int32) < live_count).astype(
                jnp.bfloat16
            )
            part_solved = part_solved * keep_mask[:, None, None]
            return running + jnp.einsum(
                "kab,kbr->ar", part_factor, part_solved, preferred_element_type=jnp.float32
            )

        start_sum = jnp.zeros((block_rows, column_count), jnp.float32)
        return lax.fori_loop(0, turn_count, add_slots, start_sum)

    def solve(target, pieces):
        corrected = (target - update(pieces)).astype(jnp.bfloat16)
        return jnp.dot(diag_inverse, corrected, preferred_element_type=jnp.float32).astype(
            jnp.bfloat16
        )

    def sweep_step(position, solved):
        carried = shifted(solved, "group", 1)
        pieces = lax.all_gather(carried, "blk", axis=0, tiled=True)
        return solve(reduced, pieces)

    start_solved = jnp.zeros((block_rows, column_total), jnp.bfloat16)
    solved = lax.fori_loop(0, group_count, sweep_step, start_solved)
    return (solved[None], local_sol.reshape(1, sub_blocks * block_rows, column_total))


def solution(mesh):
    placed = (
        P("group", "blk", None),
        P("group", "blk", None, None),
        P("group", "blk", None, None),
        P("group", "blk"),
        P("group", "blk"),
        P("group", "blk", None),
        P("group", "blk", None, None),
        P("group", "blk", None, None),
    )
    return jax.shard_map(
        on_device,
        mesh=mesh,
        in_specs=placed,
        out_specs=(P("group", "blk", None), P("group", "blk", None)),
        check_vma=False,
    )
```

profile of v0, /device:TPU:25, one launch (start us, length us, event | category | flops | bytes accessed | tf_op | source)
XLA Modules:
  0.0 750.0 jit_solution(5200894559587846281)
XLA Ops:
  8.8 3.3 convolution_convert_fusion.1
  12.2 2.3 fusion.8
  14.7 727.7 %while.21 = (s32[]{:T(128)}, bf16[128,256]{0,1:T(8,128)(2,1)S(1)}, s32[16]{0:T(128)S(1)}, s32[]{:T(128)}, bf16[16,128,128]{2,1,0:T(8,128)(2,1)}, /*index=5*/s32[...) while((s32[]{:T(128)}, bf16[128,256]{0,1:T(8,128)(2,1)S(1)}, ...), condition=%wide.region_3.4_spmd, body=%wide.region_0.3_spmd.sunk | while | flops 75891792 | bytes 14850304 | solution.py:66
  14.8 1.3 collective-permute-start
  16.1 2.0 collective-permute-done
  18.8 76.8 %all-gather.2.cloned.1.call-done = bf16[4096,256]{0,1:T(8,128)(2,1)} async-done(((bf16[128,256]{0,1:T(8,128)(2,1)}), bf16[4096,256]{0,1:T(8,128)(2,1)}) %all-gather.2.cloned.1.call-update) | async-done | bytes 2097168 | tf_op jit(solution)/shard_map/while/body/eval_jaxpr/all_gather | solution.py:62
  95.6 4.1 copy.21
  99.6 2.2 gather_fusion
  101.9 3.9 while.22
  106.0 1.3 collective-permute-start
  107.3 5.1 collective-permute-done
  113.1 73.4 %all-gather.2.cloned.1.call-done = bf16[4096,256]{0,1:T(8,128)(2,1)} async-done(((bf16[128,256]{0,1:T(8,128)(2,1)}), bf16[4096,256]{0,1:T(8,128)(2,1)}) %all-gather.2.cloned.1.call-update) | async-done | bytes 2097168 | tf_op jit(solution)/shard_map/while/body/eval_jaxpr/all_gather | solution.py:62
  186.5 4.1 copy.21
  190.6 2.2 gather_fusion
  192.8 3.9 while.22
  197.0 1.3 collective-permute-start
  198.3 5.1 collective-permute-done
  204.0 73.4 %all-gather.2.cloned.1.call-done = bf16[4096,256]{0,1:T(8,128)(2,1)} async-done(((bf16[128,256]{0,1:T(8,128)(2,1)}), bf16[4096,256]{0,1:T(8,128)(2,1)}) %all-gather.2.cloned.1.call-update) | async-done | bytes 2097168 | tf_op jit(solution)/shard_map/while/body/eval_jaxpr/all_gather | solution.py:62
  277.4 4.1 copy.21
  281.5 2.2 gather_fusion
  283.7 3.9 while.22
  287.9 1.3 collective-permute-start
  289.2 5.1 collective-permute-done
  294.9 73.4 %all-gather.2.cloned.1.call-done = bf16[4096,256]{0,1:T(8,128)(2,1)} async-done(((bf16[128,256]{0,1:T(8,128)(2,1)}), bf16[4096,256]{0,1:T(8,128)(2,1)}) %all-gather.2.cloned.1.call-update) | async-done | bytes 2097168 | tf_op jit(solution)/shard_map/while/body/eval_jaxpr/all_gather | solution.py:62
  368.3 4.1 copy.21
  372.4 2.2 gather_fusion
  374.6 3.9 while.22
  380.1 5.1 collective-permute-done
  385.9 73.4 %all-gather.2.cloned.1.call-done = bf16[4096,256]{0,1:T(8,128)(2,1)} async-done(((bf16[128,256]{0,1:T(8,128)(2,1)}), bf16[4096,256]{0,1:T(8,128)(2,1)}) %all-gather.2.cloned.1.call-update) | async-done | bytes 2097168 | tf_op jit(solution)/shard_map/while/body/eval_jaxpr/all_gather | solution.py:62
  459.3 4.1 copy.21
  463.3 2.2 gather_fusion
  465.6 3.9 while.22
  471.0 5.1 collective-permute-done
  476.8 73.4 %all-gather.2.cloned.1.call-done = bf16[4096,256]{0,1:T(8,128)(2,1)} async-done(((bf16[128,256]{0,1:T(8,128)(2,1)}), bf16[4096,256]{0,1:T(8,128)(2,1)}) %all-gather.2.cloned.1.call-update) | async-done | bytes 2097168 | tf_op jit(solution)/shard_map/while/body/eval_jaxpr/all_gather | solution.py:62
  550.2 4.1 copy.21
  554.3 2.2 gather_fusion
  556.5 3.9 while.22
  562.0 5.1 collective-permute-done
  567.7 73.4 %all-gather.2.cloned.1.call-done = bf16[4096,256]{0,1:T(8,128)(2,1)} async-done(((bf16[128,256]{0,1:T(8,128)(2,1)}), bf16[4096,256]{0,1:T(8,128)(2,1)}) %all-gather.2.cloned.1.call-update) | async-done | bytes 2097168 | tf_op jit(solution)/shard_map/while/body/eval_jaxpr/all_gather | solution.py:62
  641.1 4.1 copy.21
  645.2 2.2 gather_fusion
  647.4 3.9 while.22
  651.6 1.3 collective-permute-start
  652.9 5.1 collective-permute-done
  658.6 73.4 %all-gather.2.cloned.1.call-done = bf16[4096,256]{0,1:T(8,128)(2,1)} async-done(((bf16[128,256]{0,1:T(8,128)(2,1)}), bf16[4096,256]{0,1:T(8,128)(2,1)}) %all-gather.2.cloned.1.call-update) | async-done | bytes 2097168 | tf_op jit(solution)/shard_map/while/body/eval_jaxpr/all_gather | solution.py:62
  732.0 4.1 copy.21
  736.1 2.2 gather_fusion
  738.3 3.9 while.22
  (113 shorter events, 43.5 us)
Async XLA Ops:
  7.2 1.6 copy-start
  8.8 3.3 copy-start.4
  8.8 3.4 copy-start.2
  12.1 2.6 copy-start.3
  12.1 2.6 copy-start.5
  14.7 80.8 %all-gather.2.cloned.1.call-start = ((), (), s32[]{:S(2)}) async-start(), calls=%async_computation | async-start | bytes 2162688 | tf_op jit(solution)/shard_map/while/body/eval_jaxpr/all_gather | solution.py:62
  14.8 3.3 collective-permute-start
  18.1 0.6 copy-start.1
  106.0 80.5 %all-gather.2.cloned.1.call-start = ((), (), s32[]{:S(2)}) async-start(), calls=%async_computation | async-start | bytes 2162688 | tf_op jit(solution)/shard_map/while/body/eval_jaxpr/all_gather | solution.py:62
  106.0 6.4 collective-permute-start
  112.4 0.6 copy-start.1
  196.9 80.5 %all-gather.2.cloned.1.call-start = ((), (), s32[]{:S(2)}) async-start(), calls=%async_computation | async-start | bytes 2162688 | tf_op jit(solution)/shard_map/while/body/eval_jaxpr/all_gather | solution.py:62
  197.0 6.4 collective-permute-start
  203.3 0.6 copy-start.1
  287.8 80.5 %all-gather.2.cloned.1.call-start = ((), (), s32[]{:S(2)}) async-start(), calls=%async_computation | async-start | bytes 2162688 | tf_op jit(solution)/shard_map/while/body/eval_jaxpr/all_gather | solution.py:62
  287.9 6.4 collective-permute-start
  294.3 0.6 copy-start.1
  378.8 80.5 %all-gather.2.cloned.1.call-start = ((), (), s32[]{:S(2)}) async-start(), calls=%async_computation | async-start | bytes 2162688 | tf_op jit(solution)/shard_map/while/body/eval_jaxpr/all_gather | solution.py:62
  378.8 6.4 collective-permute-start
  385.2 0.6 copy-start.1
  469.7 80.5 %all-gather.2.cloned.1.call-start = ((), (), s32[]{:S(2)}) async-start(), calls=%async_computation | async-start | bytes 2162688 | tf_op jit(solution)/shard_map/while/body/eval_jaxpr/all_gather | solution.py:62
  469.7 6.4 collective-permute-start
  476.1 0.6 copy-start.1
  560.6 80.5 %all-gather.2.cloned.1.call-start = ((), (), s32[]{:S(2)}) async-start(), calls=%async_computation | async-start | bytes 2162688 | tf_op jit(solution)/shard_map/while/body/eval_jaxpr/all_gather | solution.py:62
  560.7 6.4 collective-permute-start
  567.0 0.6 copy-start.1
  651.5 80.5 %all-gather.2.cloned.1.call-start = ((), (), s32[]{:S(2)}) async-start(), calls=%async_computation | async-start | bytes 2162688 | tf_op jit(solution)/shard_map/while/body/eval_jaxpr/all_gather | solution.py:62
  651.6 6.4 collective-permute-start
  658.0 0.6 copy-start.1
Sparse Core Ops, SparseCore 0:
  18.9 76.6 all-gather.1
  113.2 73.2 all-gather.1
  204.1 73.2 all-gather.1
  295.0 73.2 all-gather.1
  386.0 73.2 all-gather.1
  476.9 73.2 all-gather.1
  567.8 73.2 all-gather.1
  658.7 73.2 all-gather.1
where the time goes:
time: 755 us; the launch traced here: 750 us
  waiting for transfers between devices  628 us (83%)
  local copies, waits for them, and re-layouts  57 us (8%)
  matrix products  27.5 us (4%)
  between operations  14.9 us (2%)
  starting transfers between devices  10.7 us (1%)
  other arithmetic  10.5 us (1%)
    all_gather x8, waiting for transfers between devices, sweep_step(): pieces = lax.all_gather(carried, 'blk', axis=0, tiled=True)  590 us
    ppermute x8, waiting for transfers between devices, shifted(): lax.ppermute(value, axis, [(source, source + steps) for source in range(f...  37.6 us
    all_gather x8, local copies, waits for them, and re-layouts, sweep_step(): pieces = lax.all_gather(carried, 'blk', axis=0, tiled=True)  32.6 us
    dot_general x16, matrix products, add_slots(): jnp.einsum('kab,kbr->ar', part_factor, part_solved, preferred_element_typ...  20.2 us
    gather x8, local copies, waits for them, and re-layouts, update(): chosen = pieces.reshape(owners, block_rows, column_count)[sources]  17.6 us
  transfers between devices with their start and end apart: 16, of which 16 were waited for; matrix products, arithmetic and copies ran while one was open for 0% of the time, Pallas kernels for 0%

commit v1 on v0

v1 whole, which is shorter than its diff:
```python
import jax
import jax.numpy as jnp
from jax import lax
from jax.experimental import pallas as pl
from jax.experimental.pallas import tpu as pltpu
from jax.sharding import PartitionSpec as P

MESH = pl.DeviceIdType.MESH
F32, BF16, I32 = jnp.float32, jnp.bfloat16, jnp.int32

GROUPS = 8
CORES = 2
RINGS = GROUPS // CORES
XS, ZS = 4, 8
OWNERS = XS * ZS
BLOCK = 128
COLUMNS = 256
CHUNK = COLUMNS // GROUPS
HALVES = 2
HALF = CHUNK // HALVES
SLOTS = 16
SUBS = 32
LOADS = 8
PER = SUBS // LOADS

NT = (((1,), (1,)), ((), ()))


def ring(step, size):
    return min(step, size - step)


OFFSETS = sorted(
    ((dx, dz) for dx in range(XS) for dz in range(ZS) if (dx, dz) != (0, 0)),
    key=lambda p: -(ring(p[0], XS) + ring(p[1], ZS)),
)


def kernel(
    sep_rhs, sep_inv, fac, src, count, sub_rhs, sub_inv, sub_coup,
    sep_out, sub_out,
    rhs_v, inv_v, coup_v, sol_v, sep_v, red_t, red_all, low_all, fac_all,
    src_v, count_s, idx_v, idx_s, home, result,
    *rest,
):
    gath = [rest[t * HALVES : (t + 1) * HALVES] for t in range(GROUPS)]
    (
        load_sem, small_sem, sub_sem, red_send, red_sem, low_send, low_sem, fac_send, fac_fwd, fac_sem,
        idx_send, idx_sem, idx_local, x_send, x_sem, home_send, home_sem, out_sem,
    ) = rest[GROUPS * HALVES :]
    g, o = lax.axis_index("group"), lax.axis_index("blk")
    y, core = g // CORES, lax.rem(g, CORES)
    x, z = o // ZS, lax.rem(o, ZS)

    def owner(dx, dz):
        return {"blk": lax.rem(x + dx, XS) * ZS + lax.rem(z + dz, ZS)}

    def group_peer(d):
        return {"group": lax.rem(g + d, GROUPS)}

    def y_peer(d):
        return {"group": lax.rem(y + d, RINGS) * CORES + core}

    sibling = {"group": y * CORES + 1 - core}

    def remote(source, target, send, recv, device):
        return pltpu.make_async_remote_copy(
            src_ref=source, dst_ref=target, send_sem=send, recv_sem=recv,
            device_id=device, device_id_type=MESH,
        )

    def drain(ref, sem):
        pltpu.make_async_copy(ref, ref, sem).wait()

    rows = PER * BLOCK

    def loads(c):
        part, blocks = pl.ds(c * rows, rows), pl.ds(c * PER, PER)
        return (
            pltpu.make_async_copy(sub_rhs.at[0, part], rhs_v.at[part], load_sem.at[0, c]),
            pltpu.make_async_copy(sub_inv.at[0, blocks], inv_v.at[blocks], load_sem.at[1, c]),
            pltpu.make_async_copy(sub_coup.at[0, blocks], coup_v.at[blocks], load_sem.at[2, c]),
        )

    for c in range(LOADS):
        for copy in loads(c):
            copy.start()
    small = (
        pltpu.make_async_copy(sep_rhs.at[0], sep_v, small_sem.at[0]),
        pltpu.make_async_copy(src, src_v, small_sem.at[1]),
        pltpu.make_async_copy(count, count_s, small_sem.at[2]),
    )
    for copy in small:
        copy.start()
    pltpu.make_async_copy(sep_inv.at[0, 0], low_all.at[g], low_sem.at[g]).start()
    pltpu.make_async_copy(fac.at[0], fac_all.at[g], fac_sem.at[g]).start()

    barrier = pltpu.get_barrier_semaphore()
    for dx, dz in OFFSETS:
        pl.semaphore_signal(barrier, inc=1, device_id=owner(dx, dz), device_id_type=MESH)
    for d in range(1, GROUPS):
        pl.semaphore_signal(barrier, inc=1, device_id=group_peer(d), device_id_type=MESH)

    for t in range(GROUPS - 1):
        for h in range(HALVES):
            gath[t][h][OWNERS] = jnp.zeros((HALF, BLOCK), BF16)
    for copy in small:
        copy.wait()
    slot = lax.broadcasted_iota(I32, (1, SLOTS), 1)
    idx_v[g] = jnp.zeros((1, BLOCK), I32)
    idx_v[g, :, pl.ds(0, SLOTS)] = jnp.where(slot < count_s[0, 0], src_v[...], OWNERS)

    def subtree(c, total):
        for copy in loads(c):
            copy.wait()
        solved = []
        for i in range(PER):
            n = c * PER + i
            part = pl.ds(pl.multiple_of(n * BLOCK, BLOCK), BLOCK)
            sol = jnp.dot(inv_v[n], rhs_v[part, :], preferred_element_type=F32).astype(BF16)
            sol_v[part, :] = sol
            solved.append(sol)
        part = pl.ds(pl.multiple_of(c * rows, rows), rows)
        pltpu.make_async_copy(sol_v.at[part], sub_out.at[0, part], sub_sem.at[c]).start()
        coup = jnp.concatenate([coup_v[c * PER + i] for i in range(PER)], axis=1)
        return total + jnp.dot(coup, jnp.concatenate(solved, axis=0), preferred_element_type=F32)

    lifted = lax.fori_loop(0, LOADS, subtree, jnp.zeros((BLOCK, COLUMNS), F32))
    red_t[...] = jnp.transpose(sep_v[...] - lifted).reshape(GROUPS, CHUNK, BLOCK)

    pl.semaphore_wait(barrier, len(OFFSETS) + GROUPS - 1)

    pltpu.make_async_copy(red_t.at[g], red_all.at[g], red_sem.at[g]).start()
    for d in (4, 5, 3, 6, 2, 7, 1):
        peer = group_peer(d)
        remote(red_t.at[peer["group"]], red_all.at[g], red_send, red_sem.at[g], peer).start()
        remote(sep_inv.at[0, 0], low_all.at[g], low_send, low_sem.at[g], peer).start()
    for d in range(1, GROUPS):
        remote(idx_v.at[g], idx_v.at[g], idx_send, idx_sem.at[g], group_peer(d)).start()

    def send_factors():
        for d in (2, 1, 3):
            remote(fac.at[0], fac_all.at[g], fac_send.at[d], fac_sem.at[g], y_peer(d)).start()
        remote(fac.at[0], fac_all.at[g], fac_send.at[0], fac_sem.at[g], sibling).start()

    early = 4

    @pl.when((g >= 1) & (g < early))
    def _():
        send_factors()

    def forwards(t):
        return (core == t % CORES) & (y != t // CORES)

    def pass_on(t):
        @pl.when(forwards(t))
        def _():
            drain(fac_all.at[t], fac_sem.at[t])
            remote(fac_all.at[t], fac_all.at[t], fac_fwd.at[t], fac_sem.at[t], sibling).start()

    drain(red_all.at[0], red_sem.at[0])
    drain(low_all.at[0], low_sem.at[0])
    for t in range(GROUPS):
        if t == 1:
            for other in range(GROUPS):
                @pl.when(g != other)
                def _():
                    drain(idx_v.at[other], idx_sem.at[other])
            copy = pltpu.make_async_copy(idx_v, idx_s, idx_local)
            copy.start()
            copy.wait()
        if t:
            drain(red_all.at[t], red_sem.at[t])
            drain(low_all.at[t], low_sem.at[t])

            @pl.when(jnp.logical_not(forwards(t)))
            def _():
                drain(fac_all.at[t], fac_sem.at[t])

        for h in range(HALVES):
            target = red_all[t, pl.ds(h * HALF, HALF), :]
            if t:
                before = gath[t - 1][h]
                drain(before.at[pl.ds(0, OWNERS - 1)], x_sem.at[t - 1, h])
                chosen = jnp.concatenate([before[idx_s[t, 0, k]] for k in range(SLOTS)], axis=1)
                factors = jnp.concatenate([fac_all[t, k] for k in range(SLOTS)], axis=1)
                target = target - lax.dot_general(chosen, factors, NT, preferred_element_type=F32)
            solved = lax.dot_general(
                target.astype(BF16), low_all[t], NT, preferred_element_type=F32
            ).astype(BF16)
            mine = gath[t][h]
            mine[o] = solved
            if t < GROUPS - 1:
                for dx, dz in OFFSETS:
                    remote(
                        mine.at[o], mine.at[o], x_send.at[t, h], x_sem.at[t, h], owner(dx, dz)
                    ).start()

            @pl.when(g == t)
            def _():
                pltpu.make_async_copy(mine.at[o], home.at[g, h], home_sem).start()

            @pl.when(g != t)
            def _():
                remote(
                    mine.at[o], home.at[g, h], home_send.at[t, h], home_sem, {"group": t}
                ).start()

        if t == 0:
            @pl.when(g >= early)
            def _():
                send_factors()
        if t < GROUPS - 1:
            pass_on(t + 1)

    drain(home, home_sem)
    whole = home[...].reshape(COLUMNS, BLOCK).astype(F32)
    result[...] = jnp.transpose(whole).astype(BF16)
    out = pltpu.make_async_copy(result, sep_out.at[0], out_sem)
    out.start()

    for c in range(LOADS):
        part = pl.ds(c * rows, rows)
        pltpu.make_async_copy(sol_v.at[part], sub_out.at[0, part], sub_sem.at[c]).wait()
    drain(red_t.at[pl.ds(0, GROUPS - 1)], red_send)
    drain(low_all.at[pl.ds(0, GROUPS - 1)], low_send)
    drain(idx_v.at[pl.ds(0, GROUPS - 1)], idx_send)

    @pl.when(g >= 1)
    def _():
        for d in range(RINGS):
            drain(fac_all.at[0], fac_send.at[d])

    @pl.when(g == 0)
    def _():
        drain(fac_all.at[0], fac_sem.at[0])

    for t in range(1, GROUPS):
        @pl.when(forwards(t))
        def _():
            drain(fac_all.at[t], fac_fwd.at[t])
    for t in range(GROUPS):
        for h in range(HALVES):
            if t < GROUPS - 1:
                drain(gath[t][h].at[pl.ds(0, OWNERS - 1)], x_send.at[t, h])

            @pl.when(g != t)
            def _():
                drain(gath[t][h].at[0], home_send.at[t, h])
    out.wait()


def on_device(*args):
    dma = pltpu.SemaphoreType.DMA
    scratch = [
        pltpu.VMEM((SUBS * BLOCK, COLUMNS), BF16),
        pltpu.VMEM((SUBS, BLOCK, BLOCK), BF16),
        pltpu.VMEM((SUBS, BLOCK, BLOCK), BF16),
        pltpu.VMEM((SUBS * BLOCK, COLUMNS), BF16),
        pltpu.VMEM((BLOCK, COLUMNS), F32),
        pltpu.VMEM((GROUPS, CHUNK, BLOCK), F32),
        pltpu.VMEM((GROUPS, CHUNK, BLOCK), F32),
        pltpu.VMEM((GROUPS, BLOCK, BLOCK), BF16),
        pltpu.VMEM((GROUPS, SLOTS, BLOCK, BLOCK), BF16),
        pltpu.VMEM((1, SLOTS), I32),
        pltpu.SMEM((1, 1), I32),
        pltpu.VMEM((GROUPS, 1, BLOCK), I32),
        pltpu.SMEM((GROUPS, 1, BLOCK), I32),
        pltpu.VMEM((GROUPS, HALVES, HALF, BLOCK), BF16),
        pltpu.VMEM((BLOCK, COLUMNS), BF16),
        *[pltpu.VMEM((OWNERS + 1, HALF, BLOCK), BF16)] * (GROUPS * HALVES),
        dma((3, LOADS)), dma((3,)), dma((LOADS,)),
        dma, dma((GROUPS,)), dma, dma((GROUPS,)),
        dma((RINGS,)), dma((GROUPS,)), dma((GROUPS,)),
        dma, dma((GROUPS,)), dma,
        dma((GROUPS, HALVES)), dma((GROUPS, HALVES)), dma((GROUPS, HALVES)), dma, dma,
    ]
    return pl.pallas_call(
        kernel,
        out_shape=(
            jax.ShapeDtypeStruct((1, BLOCK, COLUMNS), BF16),
            jax.ShapeDtypeStruct((1, SUBS * BLOCK, COLUMNS), BF16),
        ),
        in_specs=[pl.BlockSpec(memory_space=pl.ANY)] * 8,
        out_specs=[pl.BlockSpec(memory_space=pl.ANY)] * 2,
        scratch_shapes=scratch,
        compiler_params=pltpu.CompilerParams(
            collective_id=0, has_side_effects=True, vmem_limit_bytes=48 << 20
        ),
    )(*args)


def solution(mesh):
    rows = P("group", "blk", None)
    blocks = P("group", "blk", None, None)
    flat = P("group", "blk")
    return jax.shard_map(
        on_device,
        mesh=mesh,
        in_specs=(rows, blocks, blocks, flat, flat, rows, blocks, blocks),
        out_specs=(rows, rows),
        check_vma=False,
    )
```

time: 755 us -> 92.1 us (0.12)
  waiting for transfers between devices: 628 us -> 0 us
  Pallas kernels: 0 us -> 82.7 us
  local copies, waits for them, and re-layouts: 57 us -> 7.75 us
  matrix products: 27.5 us -> 0 us
  between operations: 14.9 us -> 1.3 us
  starting transfers between devices: 10.7 us -> 0 us
  other arithmetic: 10.5 us -> 0 us
    all_gather x8 -> x0, waiting for transfers between devices: 590 us -> none  [sweep_step(): pieces = lax.all_gather(carried, 'blk', axis=0, tiled=True)]
    pallas_call x0 -> x1, Pallas kernels: none -> 82.7 us  [on_device(): pl.pallas_call(kernel, out_shape=(jax.ShapeDtypeStruct((1, BLOCK, COLUMNS...]
    ppermute x8 -> x0, waiting for transfers between devices: 37.6 us -> none  [shifted(): lax.ppermute(value, axis, [(source, source + steps) for source in range(f...]
    all_gather x8 -> x0, local copies, waits for them, and re-layouts: 32.6 us -> none  [sweep_step(): pieces = lax.all_gather(carried, 'blk', axis=0, tiled=True)]
    dot_general x26 -> x0, matrix products: 27.5 us -> none  [the longest x16 20.2 us: add_slots(): jnp.einsum('kab,kbr->ar', part_factor, part_solved, preferred_element_typ...]
    gather x8 -> x0, local copies, waits for them, and re-layouts: 17.6 us -> none  [update(): chosen = pieces.reshape(owners, block_rows, column_count)[sources]]
    convert_element_type x16 -> x0, other arithmetic: 10.4 us -> none  [add_slots(): (first_slot + jnp.arange(step_size, dtype=jnp.int32) < live_count).astype...]
    ppermute x8 -> x0, starting transfers between devices: 10.3 us -> none  [shifted(): lax.ppermute(value, axis, [(source, source + steps) for source in range(f...]
  transfers between devices with their start and end apart: 16 -> 0, of which waited for: 16 -> 0; matrix products, arithmetic and copies ran while one was open for 0% -> 0% of each run, Pallas kernels for 0% -> 0%
where the time goes in v1:
time: 92.1 us; the launch traced here: 91.8 us
  Pallas kernels  82.7 us (90%)
  local copies, waits for them, and re-layouts  7.75 us (8%)
  between operations  1.3 us (1%)
    pallas_call x1, Pallas kernels, on_device(): pl.pallas_call(kernel, out_shape=(jax.ShapeDtypeStruct((1, BLOCK, COLUMNS...  82.7 us
    unnamed x14, local copies, waits for them, and re-layouts  7.75 us

profile of v1, /device:TPU:25, one launch (start us, length us, event | category | flops | bytes accessed | tf_op | source)
XLA Modules:
  0.0 91.8 jit_solution(16755594926678112394)
XLA Ops:
  1.3 0.0 copy-start
  1.3 1.2 %copy-done = bf16[1,32,128,128]{3,2,1,0:T(8,128)(2,1)S(1)} copy-done((bf16[1,32,128,128]{3,2,1,0:T(8,128)(2,1)S(1)}, bf16[1,32,128,128]{3,2,1,0:T(8,128)(2,1)}, u32[]{:S(2)}) %copy-start) | copy-done | bytes 1048600
  2.5 0.0 copy-start.1
  2.5 1.2 %copy-done.1 = bf16[1,32,128,128]{3,2,1,0:T(8,128)(2,1)S(1)} copy-done((bf16[1,32,128,128]{3,2,1,0:T(8,128)(2,1)S(1)}, bf16[1,32,128,128]{3,2,1,0:T(8,128)(2,1)}, u32[]{:S(2)}) %copy-start.1) | copy-done | bytes 1048600
  3.7 0.0 copy-start.2
  3.7 1.0 %copy-done.2 = bf16[1,16,128,128]{3,2,1,0:T(8,128)(2,1)S(1)} copy-done((bf16[1,16,128,128]{3,2,1,0:T(8,128)(2,1)S(1)}, bf16[1,16,128,128]{3,2,1,0:T(8,128)(2,1)}, u32[]{:S(2)}) %copy-start.2) | copy-done | bytes 524312
  4.8 0.0 copy-start.3
  4.8 0.9 copy-done.3
  5.7 0.0 copy-start.4
  5.7 0.8 copy-done.4
  6.4 0.0 copy-start.5
  6.4 0.7 copy-done.5
  7.1 82.7 %shard_map.95 = (bf16[1,128,256]{2,1,0:T(8,128)(2,1)S(1)}, bf16[1,4096,256]{2,1,0:T(8,128)(2,1)S(1)}) custom-call(f32[1,128,256]{2,1,0:T(8,128)S(1)} %copy-done.3, bf16[1,1,128,128]{3,2,1,0:T(8,128)(2,1)S(1)} %copy-done.4, bf16[1,16,128,128]{3,2,1,0:T(8,128)(2,1)S(1)} %copy-done.2, s32[1,16]{1,0:T(1,128)S(1)} %copy-done.5, s32[1,1]{1,0:T(1,128)S(6)} %copy.12.count, ...), custom_call_target="tpu_custom_call" | custom-call | tf_op jit(solution)/shard_map/pallas_call | solution.py:278
  89.8 0.6 copy.13
  90.5 1.3 %copy.14 = bf16[1,4096,256]{2,1,0:T(8,128)(2,1)} copy(bf16[1,4096,256]{2,1,0:T(8,128)(2,1)S(1)} %get-tuple-element.5) | data formatting | bytes 4194304
Async XLA Ops:
  1.3 1.2 %copy-start = (bf16[1,32,128,128]{3,2,1,0:T(8,128)(2,1)S(1)}, bf16[1,32,128,128]{3,2,1,0:T(8,128)(2,1)}, u32[]{:S(2)}) copy-start(bf16[1,32,128,128]{3,2,1,0:T(8,128)(2,1)} %sub_inv.1) | copy-start | bytes 3145732
  2.5 1.2 %copy-start.1 = (bf16[1,32,128,128]{3,2,1,0:T(8,128)(2,1)S(1)}, bf16[1,32,128,128]{3,2,1,0:T(8,128)(2,1)}, u32[]{:S(2)}) copy-start(bf16[1,32,128,128]{3,2,1,0:T(8,128)(2,1)} %sub_coup.1) | copy-start | bytes 3145732
  3.7 1.0 %copy-start.2 = (bf16[1,16,128,128]{3,2,1,0:T(8,128)(2,1)S(1)}, bf16[1,16,128,128]{3,2,1,0:T(8,128)(2,1)}, u32[]{:S(2)}) copy-start(bf16[1,16,128,128]{3,2,1,0:T(8,128)(2,1)} %fac.1) | copy-start | bytes 1572868
  4.8 0.9 copy-start.3
  5.7 0.8 copy-start.4
  6.4 0.7 copy-start.5

commit v2 on v1

v2 whole, which is shorter than its diff:
```python
import jax
import jax.numpy as jnp
from jax import lax
from jax.experimental import pallas as pl
from jax.experimental.pallas import tpu as pltpu
from jax.sharding import PartitionSpec as P

MESH = pl.DeviceIdType.MESH
F32, BF16, I32 = jnp.float32, jnp.bfloat16, jnp.int32

GROUPS = 8
CORES = 2
RINGS = GROUPS // CORES
XS, ZS = 4, 8
OWNERS = XS * ZS
BLOCK = 128
COLUMNS = 256
CHUNK = COLUMNS // GROUPS
HALVES = 2
HALF = CHUNK // HALVES
SLOTS = 16
SUBS = 32
LOADS = 8
PER = SUBS // LOADS

PARTS = ((0, SLOTS // 2), (SLOTS // 2, SLOTS // 2))

NT = (((1,), (1,)), ((), ()))


def ring(step, size):
    return min(step, size - step)


OFFSETS = sorted(
    ((dx, dz) for dx in range(XS) for dz in range(ZS) if (dx, dz) != (0, 0)),
    key=lambda p: -(ring(p[0], XS) + ring(p[1], ZS)),
)


def kernel(
    sep_rhs, sep_inv, fac, src, count, sub_rhs, sub_inv, sub_coup,
    sep_out, sub_out,
    rhs_v, inv_v, coup_v, sol_v, sep_v, low_v, first_t, red_t, red_all, fac_all,
    src_v, count_s, idx_v, idx_s, home, result,
    *rest,
):
    gath = [rest[t * HALVES : (t + 1) * HALVES] for t in range(GROUPS)]
    (
        load_sem, small_sem, sub_sem, first_send, first_sem, red_send, red_sem, fac_send, fac_fwd, fac_sem,
        idx_send, idx_sem, idx_local, x_send, x_sem, home_send, home_sem, out_sem,
    ) = rest[GROUPS * HALVES :]
    g, o = lax.axis_index("group"), lax.axis_index("blk")
    y, core = g // CORES, lax.rem(g, CORES)
    x, z = o // ZS, lax.rem(o, ZS)

    def owner(dx, dz):
        return {"blk": lax.rem(x + dx, XS) * ZS + lax.rem(z + dz, ZS)}

    def group_peer(d):
        return {"group": lax.rem(g + d, GROUPS)}

    def y_peer(d):
        return {"group": lax.rem(y + d, RINGS) * CORES + core}

    sibling = {"group": y * CORES + 1 - core}

    def remote(source, target, send, recv, device):
        return pltpu.make_async_remote_copy(
            src_ref=source, dst_ref=target, send_sem=send, recv_sem=recv,
            device_id=device, device_id_type=MESH,
        )

    def drain(ref, sem):
        pltpu.make_async_copy(ref, ref, sem).wait()

    barrier = pltpu.get_barrier_semaphore()
    for dx, dz in OFFSETS:
        pl.semaphore_signal(barrier, inc=1, device_id=owner(dx, dz), device_id_type=MESH)
    for d in range(1, GROUPS):
        pl.semaphore_signal(barrier, inc=1, device_id=group_peer(d), device_id_type=MESH)

    rows = PER * BLOCK

    def loads(c):
        part, blocks = pl.ds(c * rows, rows), pl.ds(c * PER, PER)
        return (
            pltpu.make_async_copy(sub_rhs.at[0, part], rhs_v.at[part], load_sem.at[0, c]),
            pltpu.make_async_copy(sub_inv.at[0, blocks], inv_v.at[blocks], load_sem.at[1, c]),
            pltpu.make_async_copy(sub_coup.at[0, blocks], coup_v.at[blocks], load_sem.at[2, c]),
        )

    for c in range(LOADS):
        for copy in loads(c):
            copy.start()
    small = (
        pltpu.make_async_copy(sep_rhs.at[0], sep_v, small_sem.at[0]),
        pltpu.make_async_copy(src, src_v, small_sem.at[1]),
        pltpu.make_async_copy(count, count_s, small_sem.at[2]),
        pltpu.make_async_copy(sep_inv.at[0, 0], low_v, small_sem.at[3]),
    )
    for copy in small:
        copy.start()
    def pieces(p):
        first, size = PARTS[p]
        some = pl.ds(first, size)
        two = [(fac.at[0, some], fac_all.at[g, some])]
        return two + [(sep_inv.at[0, 0], fac_all.at[g, SLOTS])] * p

    def fac_part(t, p):
        first, size = PARTS[p]
        return fac_all.at[t, pl.ds(first, size + p)]

    for p in range(2):
        for source, target in pieces(p):
            pltpu.make_async_copy(source, target, fac_sem.at[p, g]).start()

    for t in range(GROUPS - 1):
        for h in range(HALVES):
            gath[t][h][OWNERS] = jnp.zeros((HALF, BLOCK), BF16)
    for copy in small:
        copy.wait()
    slot = lax.broadcasted_iota(I32, (1, SLOTS), 1)
    idx_v[0] = jnp.zeros((1, BLOCK), I32)
    idx_v[g] = jnp.zeros((1, BLOCK), I32)
    idx_v[g, :, pl.ds(0, SLOTS)] = jnp.where(slot < count_s[0, 0], src_v[...], OWNERS)

    def subtree(c, total):
        for copy in loads(c):
            copy.wait()
        solved = []
        for i in range(PER):
            n = c * PER + i
            part = pl.ds(pl.multiple_of(n * BLOCK, BLOCK), BLOCK)
            sol = jnp.dot(inv_v[n], rhs_v[part, :], preferred_element_type=F32).astype(BF16)
            sol_v[part, :] = sol
            solved.append(sol)
        part = pl.ds(pl.multiple_of(c * rows, rows), rows)
        pltpu.make_async_copy(sol_v.at[part], sub_out.at[0, part], sub_sem.at[c]).start()
        coup = jnp.concatenate([coup_v[c * PER + i] for i in range(PER)], axis=1)
        return total + jnp.dot(coup, jnp.concatenate(solved, axis=0), preferred_element_type=F32)

    lifted = lax.fori_loop(0, LOADS, subtree, jnp.zeros((BLOCK, COLUMNS), F32))
    reduced = sep_v[...] - lifted
    red_t[...] = jnp.transpose(reduced).reshape(GROUPS, CHUNK, BLOCK)
    @pl.when(g == 0)
    def _():
        first = jnp.dot(low_v[...], reduced.astype(BF16), preferred_element_type=F32)
        first_t[...] = jnp.transpose(first).astype(BF16).reshape(GROUPS, HALVES, HALF, BLOCK)
        result[...] = first.astype(BF16)

    pl.semaphore_wait(barrier, len(OFFSETS) + GROUPS - 1)

    @pl.when(g == 0)
    def _():
        for h in range(HALVES):
            for d in (4, 5, 3, 2, 6, 7, 1):
                remote(
                    first_t.at[d, h], gath[0][h].at[o], first_send, first_sem.at[h], {"group": d}
                ).start()
            pltpu.make_async_copy(first_t.at[0, h], gath[0][h].at[o], first_sem.at[h]).start()

    def send_reduced():
        pltpu.make_async_copy(red_t.at[g], red_all.at[g], red_sem.at[g]).start()
        for d in (4, 5, 3, 6, 2, 7, 1):
            peer = group_peer(d)
            remote(red_t.at[peer["group"]], red_all.at[g], red_send, red_sem.at[g], peer).start()

    def send_factors():
        def to(d, p):
            for source, target in pieces(p):
                peer = y_peer(d) if d else sibling
                remote(source, target, fac_send.at[p, d], fac_sem.at[p, g], peer).start()

        to(3, 1)
        to(1, 1)

        @pl.when(g == 1)
        def _():
            to(2, 0)

        to(3, 0)
        to(1, 0)
        to(0, 1)
        to(0, 0)

    def send_indices():
        for d in range(1, GROUPS):
            remote(idx_v.at[g], idx_v.at[g], idx_send, idx_sem.at[g], group_peer(d)).start()

    def send_ahead(t):
        @pl.when(g == t)
        def _():
            send_reduced()

        if t == 1:
            @pl.when(g >= 1)
            def _():
                send_indices()

    def send_factors_of(t, until):
        @pl.when((g >= t) & (g < until))
        def _():
            send_factors()

    def forwards(t):
        return (core == t % CORES) & (y != t // CORES)

    def relays(t):
        return (core == t % CORES) & (y == (t // CORES - 1) % RINGS)

    def relayed(t):
        return (1,) if t == 1 else (1, 0)

    def forward(t, relay):
        for p in (1, 0):
            drain(fac_part(t, p), fac_sem.at[p, t])
            if relay and p in relayed(t):
                remote(
                    fac_part(t, p), fac_part(t, p), fac_fwd.at[1, p, t], fac_sem.at[p, t], y_peer(RINGS - 1)
                ).start()
            remote(fac_part(t, p), fac_part(t, p), fac_fwd.at[0, p, t], fac_sem.at[p, t], sibling).start()

    def pass_on(step):
        for t in range(1, GROUPS):
            if max(0, t - 2) == step:
                @pl.when(relays(t))
                def _():
                    forward(t, True)

        if step + 1 < GROUPS:
            @pl.when(forwards(step + 1) & jnp.logical_not(relays(step + 1)))
            def _():
                forward(step + 1, False)

    send_ahead(1)
    send_ahead(2)
    send_factors_of(1, 3)

    def spread(t, h):
        mine = gath[t][h]
        for dx, dz in OFFSETS:
            remote(mine.at[o], mine.at[o], x_send.at[t, h], x_sem.at[t, h], owner(dx, dz)).start()

    for t in range(GROUPS):
        if t == 1:
            for other in range(1, GROUPS):
                @pl.when(g != other)
                def _():
                    drain(idx_v.at[other], idx_sem.at[other])
            copy = pltpu.make_async_copy(idx_v, idx_s, idx_local)
            copy.start()
            copy.wait()
        if t:
            drain(red_all.at[t], red_sem.at[t])

            @pl.when(jnp.logical_not(forwards(t)))
            def _():
                for p in range(2):
                    drain(fac_part(t, p), fac_sem.at[p, t])

        for h in range(HALVES):
            mine = gath[t][h]
            if t == 0:
                drain(mine.at[o], first_sem.at[h])
                spread(t, h)
                continue
            before = gath[t - 1][h]
            drain(before.at[pl.ds(0, OWNERS - 1)], x_sem.at[t - 1, h])
            chosen = jnp.concatenate([before[idx_s[t, 0, k]] for k in range(SLOTS)], axis=1)
            factors = jnp.concatenate([fac_all[t, k] for k in range(SLOTS)], axis=1)
            coupling = lax.dot_general(chosen, factors, NT, preferred_element_type=F32)
            corrected = (red_all[t, pl.ds(h * HALF, HALF), :] - coupling).astype(BF16)
            solved = lax.dot_general(corrected, fac_all[t, SLOTS], NT, preferred_element_type=F32)
            mine[o] = solved.astype(BF16)
            if t < GROUPS - 1:
                spread(t, h)

            @pl.when(g == t)
            def _():
                pltpu.make_async_copy(mine.at[o], home.at[g, h], home_sem).start()

            @pl.when(g != t)
            def _():
                remote(
                    mine.at[o], home.at[g, h], home_send.at[t, h], home_sem, {"group": t}
                ).start()

        if t + 3 < GROUPS:
            send_ahead(t + 3)
            send_factors_of(t + 3, t + 4)
        if t < GROUPS - 1:
            pass_on(t)

    @pl.when(g >= 1)
    def _():
        drain(home, home_sem)
        whole = home[...].reshape(COLUMNS, BLOCK).astype(F32)
        result[...] = jnp.transpose(whole).astype(BF16)

    out = pltpu.make_async_copy(result, sep_out.at[0], out_sem)
    out.start()

    for c in range(LOADS):
        part = pl.ds(c * rows, rows)
        pltpu.make_async_copy(sol_v.at[part], sub_out.at[0, part], sub_sem.at[c]).wait()

    @pl.when(g >= 1)
    def _():
        drain(red_t.at[pl.ds(0, GROUPS - 1)], red_send)
        drain(idx_v.at[pl.ds(0, GROUPS - 1)], idx_send)
        for d in (0, 1, 3):
            for p in range(2):
                drain(fac_part(0, p), fac_send.at[p, d])

    @pl.when(g == 1)
    def _():
        drain(fac_part(0, 0), fac_send.at[0, 2])

    @pl.when(g == 0)
    def _():
        drain(first_t.at[pl.ds(0, GROUPS - 1)], first_send)
        for p in range(2):
            drain(fac_part(0, p), fac_sem.at[p, 0])

    for t in range(1, GROUPS):
        @pl.when(forwards(t))
        def _():
            for p in range(2):
                drain(fac_part(t, p), fac_fwd.at[0, p, t])

        @pl.when(relays(t))
        def _():
            for p in relayed(t):
                drain(fac_part(t, p), fac_fwd.at[1, p, t])

    for t in range(GROUPS):
        for h in range(HALVES):
            if t < GROUPS - 1:
                drain(gath[t][h].at[pl.ds(0, OWNERS - 1)], x_send.at[t, h])
            if t:
                @pl.when(g != t)
                def _():
                    drain(gath[t][h].at[0], home_send.at[t, h])
    out.wait()


def on_device(*args):
    dma = pltpu.SemaphoreType.DMA
    scratch = [
        pltpu.VMEM((SUBS * BLOCK, COLUMNS), BF16),
        pltpu.VMEM((SUBS, BLOCK, BLOCK), BF16),
        pltpu.VMEM((SUBS, BLOCK, BLOCK), BF16),
        pltpu.VMEM((SUBS * BLOCK, COLUMNS), BF16),
        pltpu.VMEM((BLOCK, COLUMNS), F32),
        pltpu.VMEM((BLOCK, BLOCK), BF16),
        pltpu.VMEM((GROUPS, HALVES, HALF, BLOCK), BF16),
        pltpu.VMEM((GROUPS, CHUNK, BLOCK), F32),
        pltpu.VMEM((GROUPS, CHUNK, BLOCK), F32),
        pltpu.VMEM((GROUPS, SLOTS + 1, BLOCK, BLOCK), BF16),
        pltpu.VMEM((1, SLOTS), I32),
        pltpu.SMEM((1, 1), I32),
        pltpu.VMEM((GROUPS, 1, BLOCK), I32),
        pltpu.SMEM((GROUPS, 1, BLOCK), I32),
        pltpu.VMEM((GROUPS, HALVES, HALF, BLOCK), BF16),
        pltpu.VMEM((BLOCK, COLUMNS), BF16),
        *[pltpu.VMEM((OWNERS + 1, HALF, BLOCK), BF16)] * (GROUPS * HALVES),
        dma((3, LOADS)), dma((4,)), dma((LOADS,)),
        dma, dma((HALVES,)), dma, dma((GROUPS,)),
        dma((2, RINGS)), dma((2, 2, GROUPS)), dma((2, GROUPS)),
        dma, dma((GROUPS,)), dma,
        dma((GROUPS, HALVES)), dma((GROUPS, HALVES)), dma((GROUPS, HALVES)), dma, dma,
    ]
    return pl.pallas_call(
        kernel,
        out_shape=(
            jax.ShapeDtypeStruct((1, BLOCK, COLUMNS), BF16),
            jax.ShapeDtypeStruct((1, SUBS * BLOCK, COLUMNS), BF16),
        ),
        in_specs=[pl.BlockSpec(memory_space=pl.ANY)] * 8,
        out_specs=[pl.BlockSpec(memory_space=pl.ANY)] * 2,
        scratch_shapes=scratch,
        compiler_params=pltpu.CompilerParams(
            collective_id=0, has_side_effects=True, vmem_limit_bytes=48 << 20
        ),
    )(*[a if i == 4 else pltpu.with_memory_space_constraint(a, pltpu.HBM) for i, a in enumerate(args)])


def solution(mesh):
    rows = P("group", "blk", None)
    blocks = P("group", "blk", None, None)
    flat = P("group", "blk")
    return jax.shard_map(
        on_device,
        mesh=mesh,
        in_specs=(rows, blocks, blocks, flat, flat, rows, blocks, blocks),
        out_specs=(rows, rows),
        check_vma=False,
    )
```

time: 92.1 us -> 77.6 us (0.84)
  Pallas kernels: 82.7 us -> 74.3 us
  local copies, waits for them, and re-layouts: 7.75 us -> 1.95 us
    pallas_call x1, Pallas kernels: 82.7 us -> 74.3 us  [on_device(): pl.pallas_call(kernel, out_shape=(jax.ShapeDtypeStruct((1, BLOCK, COLUMNS...]
    unnamed x14 -> x2, local copies, waits for them, and re-layouts: 7.75 us -> 1.95 us
where the time goes in v2:
time: 77.6 us; the launch traced here: 77.5 us
  Pallas kernels  74.3 us (96%)
  local copies, waits for them, and re-layouts  1.95 us (3%)
  between operations  1.29 us (2%)
    pallas_call x1, Pallas kernels, on_device(): pl.pallas_call(kernel, out_shape=(jax.ShapeDtypeStruct((1, BLOCK, COLUMNS...  74.3 us
    unnamed x2, local copies, waits for them, and re-layouts  1.95 us

profile of v2, /device:TPU:25, one launch (start us, length us, event | category | flops | bytes accessed | tf_op | source)
XLA Modules:
  0.0 77.5 jit_solution(17843153528978874382)
XLA Ops:
  1.3 74.3 %shard_map.95 = (bf16[1,128,256]{2,1,0:T(8,128)(2,1)S(1)}, bf16[1,4096,256]{2,1,0:T(8,128)(2,1)S(1)}) custom-call(f32[1,128,256]{2,1,0:T(8,128)} %sep_rhs.1, bf16[1,1,128,128]{3,2,1,0:T(8,128)(2,1)} %sep_inv.1, bf16[1,16,128,128]{3,2,1,0:T(8,128)(2,1)} %fac.1, s32[1,16]{1,0:T(1,128)} %src.1, s32[1,1]{1,0:T(1,128)S(6)} %copy.12.count, ...), custom_call_target="tpu_custom_call" | custom-call | tf_op jit(solution)/shard_map/pallas_call | solution.py:374
  75.6 0.6 copy.13
  76.2 1.3 %copy.14 = bf16[1,4096,256]{2,1,0:T(8,128)(2,1)} copy(bf16[1,4096,256]{2,1,0:T(8,128)(2,1)S(1)} %get-tuple-element.5) | data formatting | bytes 4194304

commit v3 on v2

--- a/solution.py
+++ b/solution.py
@@ -20,8 +20,9 @@
 HALF = CHUNK // HALVES
 SLOTS = 16
 SUBS = 32
-LOADS = 8
+LOADS = 4
 PER = SUBS // LOADS
+MEET_AT = 2
 
 PARTS = ((0, SLOTS // 2), (SLOTS // 2, SLOTS // 2))
 
@@ -42,13 +43,13 @@
     sep_rhs, sep_inv, fac, src, count, sub_rhs, sub_inv, sub_coup,
     sep_out, sub_out,
     rhs_v, inv_v, coup_v, sol_v, sep_v, low_v, first_t, red_t, red_all, fac_all,
-    src_v, count_s, idx_v, idx_s, home, result,
+    src_v, count_s, idx_v, idx_s, home,
     *rest,
 ):
     gath = [rest[t * HALVES : (t + 1) * HALVES] for t in range(GROUPS)]
     (
         load_sem, small_sem, sub_sem, first_send, first_sem, red_send, red_sem, fac_send, fac_fwd, fac_sem,
-        idx_send, idx_sem, idx_local, x_send, x_sem, home_send, home_sem, out_sem,
+        idx_send, idx_sem, idx_local, x_send, x_sem, home_send, home_sem,
     ) = rest[GROUPS * HALVES :]
     g, o = lax.axis_index("group"), lax.axis_index("blk")
     y, core = g // CORES, lax.rem(g, CORES)
@@ -125,31 +126,75 @@
     idx_v[g] = jnp.zeros((1, BLOCK), I32)
     idx_v[g, :, pl.ds(0, SLOTS)] = jnp.where(slot < count_s[0, 0], src_v[...], OWNERS)
 
-    def subtree(c, total):
+    def send_factors(parts=(1, 0)):
+        def to(d, p):
+            for source, target in pieces(p):
+                peer = y_peer(d) if d else sibling
+                remote(source, target, fac_send.at[p, d], fac_sem.at[p, g], peer).start()
+
+        if 1 in parts:
+            to(3, 1)
+            to(1, 1)
+
+        if 0 in parts:
+            @pl.when(g == 1)
+            def _():
+                to(2, 0)
+
+            to(3, 0)
+            to(1, 0)
+            to(0, 1)
+            to(0, 0)
+
+    def send_factors_of(t, until, parts=(1, 0)):
+        @pl.when((g >= t) & (g < until))
+        def _():
+            send_factors(parts)
+
+    def send_indices():
+        for d in range(1, GROUPS):
+            remote(idx_v.at[g], idx_v.at[g], idx_send, idx_sem.at[g], group_peer(d)).start()
+
+    def solve(c):
         for copy in loads(c):
             copy.wait()
-        solved = []
         for i in range(PER):
             n = c * PER + i
-            part = pl.ds(pl.multiple_of(n * BLOCK, BLOCK), BLOCK)
-            sol = jnp.dot(inv_v[n], rhs_v[part, :], preferred_element_type=F32).astype(BF16)
-            sol_v[part, :] = sol
-            solved.append(sol)
+            own = pl.ds(pl.multiple_of(n * BLOCK, BLOCK), BLOCK)
+            sol = jnp.dot(inv_v[n], rhs_v[own, :], preferred_element_type=F32)
+            sol_v[own, :] = sol.astype(BF16)
         part = pl.ds(pl.multiple_of(c * rows, rows), rows)
         pltpu.make_async_copy(sol_v.at[part], sub_out.at[0, part], sub_sem.at[c]).start()
+
+    def lift(c, total):
+        part = pl.ds(pl.multiple_of(c * rows, rows), rows)
         coup = jnp.concatenate([coup_v[c * PER + i] for i in range(PER)], axis=1)
-        return total + jnp.dot(coup, jnp.concatenate(solved, axis=0), preferred_element_type=F32)
-
-    lifted = lax.fori_loop(0, LOADS, subtree, jnp.zeros((BLOCK, COLUMNS), F32))
+        return total + jnp.dot(coup, sol_v[part, :], preferred_element_type=F32)
+
+    def subtree(c, total):
+        total = lift(c - 1, total)
+        solve(c)
+        return total
+
+    solve(0)
+    lifted = lax.fori_loop(1, MEET_AT, subtree, jnp.zeros((BLOCK, COLUMNS), F32))
+
+    pl.semaphore_wait(barrier, len(OFFSETS) + GROUPS - 1)
+    @pl.when(g >= 1)
+    def _():
+        send_indices()
+
+    send_factors_of(1, 3, (1,))
+
+    lifted = lax.fori_loop(MEET_AT, LOADS, subtree, lifted)
+    lifted = lift(LOADS - 1, lifted)
     reduced = sep_v[...] - lifted
     red_t[...] = jnp.transpose(reduced).reshape(GROUPS, CHUNK, BLOCK)
     @pl.when(g == 0)
     def _():
         first = jnp.dot(low_v[...], reduced.astype(BF16), preferred_element_type=F32)
         first_t[...] = jnp.transpose(first).astype(BF16).reshape(GROUPS, HALVES, HALF, BLOCK)
-        result[...] = first.astype(BF16)
-
-    pl.semaphore_wait(barrier, len(OFFSETS) + GROUPS - 1)
+        sep_out[0] = first.astype(BF16)
 
     @pl.when(g == 0)
     def _():
@@ -166,42 +211,10 @@
             peer = group_peer(d)
             remote(red_t.at[peer["group"]], red_all.at[g], red_send, red_sem.at[g], peer).start()
 
-    def send_factors():
-        def to(d, p):
-            for source, target in pieces(p):
-                peer = y_peer(d) if d else sibling
-                remote(source, target, fac_send.at[p, d], fac_sem.at[p, g], peer).start()
-
-        to(3, 1)
-        to(1, 1)
-
-        @pl.when(g == 1)
-        def _():
-            to(2, 0)
-
-        to(3, 0)
-        to(1, 0)
-        to(0, 1)
-        to(0, 0)
-
-    def send_indices():
-        for d in range(1, GROUPS):
-            remote(idx_v.at[g], idx_v.at[g], idx_send, idx_sem.at[g], group_peer(d)).start()
-
     def send_ahead(t):
         @pl.when(g == t)
         def _():
             send_reduced()
-
-        if t == 1:
-            @pl.when(g >= 1)
-            def _():
-                send_indices()
-
-    def send_factors_of(t, until):
-        @pl.when((g >= t) & (g < until))
-        def _():
-            send_factors()
 
     def forwards(t):
         return (core == t % CORES) & (y != t // CORES)
@@ -235,7 +248,7 @@
 
     send_ahead(1)
     send_ahead(2)
-    send_factors_of(1, 3)
+    send_factors_of(1, 3, (0,))
 
     def spread(t, h):
         mine = gath[t][h]
@@ -292,15 +305,6 @@
         if t < GROUPS - 1:
             pass_on(t)
 
-    @pl.when(g >= 1)
-    def _():
-        drain(home, home_sem)
-        whole = home[...].reshape(COLUMNS, BLOCK).astype(F32)
-        result[...] = jnp.transpose(whole).astype(BF16)
-
-    out = pltpu.make_async_copy(result, sep_out.at[0], out_sem)
-    out.start()
-
     for c in range(LOADS):
         part = pl.ds(c * rows, rows)
         pltpu.make_async_copy(sol_v.at[part], sub_out.at[0, part], sub_sem.at[c]).wait()
@@ -334,7 +338,7 @@
             for p in relayed(t):
                 drain(fac_part(t, p), fac_fwd.at[1, p, t])
 
-    for t in range(GROUPS):
+    def sent(t):
         for h in range(HALVES):
             if t < GROUPS - 1:
                 drain(gath[t][h].at[pl.ds(0, OWNERS - 1)], x_send.at[t, h])
@@ -342,7 +346,17 @@
                 @pl.when(g != t)
                 def _():
                     drain(gath[t][h].at[0], home_send.at[t, h])
-    out.wait()
+
+    for t in range(GROUPS - 1):
+        sent(t)
+    @pl.when(g >= 1)
+    def _():
+        drain(home, home_sem)
+        whole = home[...].reshape(COLUMNS, BLOCK).astype(F32)
+        sep_out[0] = jnp.transpose(whole).astype(BF16)
+
+
+    sent(GROUPS - 1)
 
 
 def on_device(*args):
@@ -363,13 +377,12 @@
         pltpu.VMEM((GROUPS, 1, BLOCK), I32),
         pltpu.SMEM((GROUPS, 1, BLOCK), I32),
         pltpu.VMEM((GROUPS, HALVES, HALF, BLOCK), BF16),
-        pltpu.VMEM((BLOCK, COLUMNS), BF16),
         *[pltpu.VMEM((OWNERS + 1, HALF, BLOCK), BF16)] * (GROUPS * HALVES),
         dma((3, LOADS)), dma((4,)), dma((LOADS,)),
         dma, dma((HALVES,)), dma, dma((GROUPS,)),
         dma((2, RINGS)), dma((2, 2, GROUPS)), dma((2, GROUPS)),
         dma, dma((GROUPS,)), dma,
-        dma((GROUPS, HALVES)), dma((GROUPS, HALVES)), dma((GROUPS, HALVES)), dma, dma,
+        dma((GROUPS, HALVES)), dma((GROUPS, HALVES)), dma((GROUPS, HALVES)), dma,
     ]
     return pl.pallas_call(
         kernel,
@@ -378,7 +391,7 @@
             jax.ShapeDtypeStruct((1, SUBS * BLOCK, COLUMNS), BF16),
         ),
         in_specs=[pl.BlockSpec(memory_space=pl.ANY)] * 8,
-        out_specs=[pl.BlockSpec(memory_space=pl.ANY)] * 2,
+        out_specs=[pl.BlockSpec(memory_space=pltpu.VMEM), pl.BlockSpec(memory_space=pl.ANY)],
         scratch_shapes=scratch,
         compiler_params=pltpu.CompilerParams(
             collective_id=0, has_side_effects=True, vmem_limit_bytes=48 << 20

time: 77.6 us -> 74.3 us (0.957)
  Pallas kernels: 74.3 us -> 71 us
    pallas_call x1, Pallas kernels: 74.3 us -> 71 us  [on_device(): pl.pallas_call(kernel, out_shape=(jax.ShapeDtypeStruct((1, BLOCK, COLUMNS...]
where the time goes in v3:
time: 74.3 us
  Pallas kernels  71 us (96%)
  local copies, waits for them, and re-layouts  1.95 us (3%)
  between operations  1.29 us (2%)
    pallas_call x1, Pallas kernels, on_device(): pl.pallas_call(kernel, out_shape=(jax.ShapeDtypeStruct((1, BLOCK, COLUMNS...  71 us
    unnamed x2, local copies, waits for them, and re-layouts  1.95 us

profile of v3, /device:TPU:25, one launch (start us, length us, event | category | flops | bytes accessed | tf_op | source)
XLA Modules:
  0.0 74.3 jit_solution(5341232812637384520)
XLA Ops:
  1.3 71.0 %shard_map.95 = (bf16[1,128,256]{2,1,0:T(8,128)(2,1)S(1)}, bf16[1,4096,256]{2,1,0:T(8,128)(2,1)S(1)}) custom-call(f32[1,128,256]{2,1,0:T(8,128)} %sep_rhs.1, bf16[1,1,128,128]{3,2,1,0:T(8,128)(2,1)} %sep_inv.1, bf16[1,16,128,128]{3,2,1,0:T(8,128)(2,1)} %fac.1, s32[1,16]{1,0:T(1,128)} %src.1, s32[1,1]{1,0:T(1,128)S(6)} %copy.12.count, ...), custom_call_target="tpu_custom_call" | custom-call | tf_op jit(solution)/shard_map/pallas_call | solution.py:387
  72.3 0.6 copy.13
  72.9 1.3 %copy.14 = bf16[1,4096,256]{2,1,0:T(8,128)(2,1)} copy(bf16[1,4096,256]{2,1,0:T(8,128)(2,1)S(1)} %get-tuple-element.5) | data formatting | bytes 4194304

commit v4 on v3

--- a/solution.py
+++ b/solution.py
@@ -185,6 +185,7 @@
         send_indices()
 
     send_factors_of(1, 3, (1,))
+    send_factors_of(1, 2, (0,))
 
     lifted = lax.fori_loop(MEET_AT, LOADS, subtree, lifted)
     lifted = lift(LOADS - 1, lifted)
@@ -248,7 +249,7 @@
 
     send_ahead(1)
     send_ahead(2)
-    send_factors_of(1, 3, (0,))
+    send_factors_of(2, 3, (0,))
 
     def spread(t, h):
         mine = gath[t][h]

time: 74.3 us -> 74.3 us (level)
  no operation moved by 1% of the time
where the time goes in v4:
time: 74.3 us; the launch traced here: 74.2 us
  Pallas kernels  70.9 us (95%)
  local copies, waits for them, and re-layouts  1.95 us (3%)
  between operations  1.29 us (2%)
    pallas_call x1, Pallas kernels, on_device(): pl.pallas_call(kernel, out_shape=(jax.ShapeDtypeStruct((1, BLOCK, COLUMNS...  70.9 us
    unnamed x2, local copies, waits for them, and re-layouts  1.95 us

profile of v4, /device:TPU:25, one launch (start us, length us, event | category | flops | bytes accessed | tf_op | source)
XLA Modules:
  0.0 74.2 jit_solution(8221574107228641405)
XLA Ops:
  1.3 70.9 %shard_map.95 = (bf16[1,128,256]{2,1,0:T(8,128)(2,1)S(1)}, bf16[1,4096,256]{2,1,0:T(8,128)(2,1)S(1)}) custom-call(f32[1,128,256]{2,1,0:T(8,128)} %sep_rhs.1, bf16[1,1,128,128]{3,2,1,0:T(8,128)(2,1)} %sep_inv.1, bf16[1,16,128,128]{3,2,1,0:T(8,128)(2,1)} %fac.1, s32[1,16]{1,0:T(1,128)} %src.1, s32[1,1]{1,0:T(1,128)S(6)} %copy.12.count, ...), custom_call_target="tpu_custom_call" | custom-call | tf_op jit(solution)/shard_map/pallas_call | solution.py:388
  72.2 0.6 copy.13
  72.9 1.3 %copy.14 = bf16[1,4096,256]{2,1,0:T(8,128)(2,1)} copy(bf16[1,4096,256]{2,1,0:T(8,128)(2,1)S(1)} %get-tuple-element.5) | data formatting | bytes 4194304
